TPU v7x, 256 devices: a whole 4x4x8 slice. The times are simulated.
256 devices in a mesh: blk: 4 (over y_hi, core), dp: 64 (over z, x, y_lo).
Axes of the slice: x: 4, y: 4 (y_hi: 2, y_lo: 2; y = y_hi * 2 + y_lo), z: 8, core: 2. Of those that a mesh axis runs over, the one named last changes fastest.
Arguments:
- fingerprints: bfloat16 [98304, 2048], P(('blk', 'dp')), may hold values from 0 to 3, as said below
- w_first: bfloat16 [2048, 1024], replicated, may hold values from -0.3125 to 0.3125
- w_second: bfloat16 [1024, 512], replicated, may hold values from -0.0625 to 0.0625
Outputs:
- grad_first: float32 [2048, 1024], P('dp')
- grad_second: float32 [1024, 512], P('dp')
Inputs may be any that keep to these rules, and one draw needn't show every extreme that they name: `fingerprints`: Non-negative feature weights; every molecule has a third or more of its features nonzero.
All inputs are finite; a program needn't handle non-finite values.
Results may differ from a plain program's by a relative error of at most 0.003.
Values may be sent and summed in bfloat16 or wider, within the bound.
A program may use at most 64 MiB of HBM per device.

v0:
```python
import math
import jax
import jax.numpy as jnp
from jax import lax
from jax.sharding import PartitionSpec as P


def pair_tile(mine_feats, mine_embed, mine_sqn, other, width):
    other_feats = other[:, :width]
    other_embed = other[:, width:]
    other_sqn = jnp.sum(jnp.square(other_feats.astype(jnp.float32)), axis=1)
    contract = (((1,), (1,)), ((), ()))
    inter = lax.dot_general(mine_feats, other_feats, contract, preferred_element_type=jnp.float32)
    tanimoto = inter / (mine_sqn[:, None] + other_sqn[None, :] - inter)
    scale = 1.0 / math.sqrt(mine_embed.shape[1])
    pred = (
        lax.dot_general(mine_embed, other_embed, contract, preferred_element_type=jnp.float32)
        * scale
    )
    return ((pred - tanimoto).astype(jnp.bfloat16), other_embed)


def column_product(left, right):
    return lax.dot_general(
        left, right, (((0,), (0,)), ((), ())), preferred_element_type=jnp.float32
    )


def per_device(fingerprints, w_first, w_second):
    tok_rows, width = fingerprints.shape
    blk_count = lax.axis_size("blk")
    dp_count = lax.axis_size("dp")
    group_rows = tok_rows * blk_count
    all_rows = group_rows * dp_count
    pre = jnp.dot(fingerprints, w_first, preferred_element_type=jnp.float32)
    sig = jax.nn.sigmoid(pre)
    hidden = (pre * sig).astype(jnp.bfloat16)
    embed = jnp.dot(hidden, w_second, preferred_element_type=jnp.float32).astype(jnp.bfloat16)
    mine_sqn = jnp.sum(jnp.square(fingerprints.astype(jnp.float32)), axis=1)
    packed = jnp.concatenate([fingerprints, embed], axis=1)
    resid, other_embed = pair_tile(
        fingerprints, embed, mine_sqn, lax.all_gather(packed, "blk", axis=0, tiled=True), width
    )
    summed = jnp.dot(resid, other_embed, preferred_element_type=jnp.float32)
    dembed = (summed * (2.0 / math.sqrt(group_rows * all_rows))).astype(jnp.bfloat16)
    dhidden = lax.dot_general(
        dembed, w_second, (((1,), (1,)), ((), ())), preferred_element_type=jnp.float32
    )
    dpre = (dhidden * sig * (1.0 + pre * (1.0 - sig))).astype(jnp.bfloat16)
    first_part = lax.psum_scatter(
        column_product(fingerprints, dpre), "dp", scatter_dimension=0, tiled=True
    )
    second_part = lax.psum_scatter(
        column_product(hidden, dembed), "dp", scatter_dimension=0, tiled=True
    )
    grad_first, grad_second = lax.psum((first_part, second_part), "blk")
    return (grad_first, grad_second)


def solution(mesh):
    in_specs = (P(("blk", "dp"), None), P(), P())
    out_specs = (P("dp", None), P("dp", None))
    return jax.shard_map(
        per_device, mesh=mesh, in_specs=in_specs, out_specs=out_specs, check_vma=False
    )
```

profile of v0, /device:TPU:1, one launch (start us, length us, event | category | flops | bytes accessed | tf_op | source)
XLA Modules:
  0.0 816.7 jit_solution(17026861810282639801)
XLA Ops:
  7.2 0.0 copy-start
  7.2 0.0 all-gather.2.cloned.1.call-start
  7.2 4.5 fusion.22
  11.8 0.0 copy-start.2
  11.8 1.1 copy-done.2
  12.9 0.0 copy-done
  12.9 0.0 copy-start.1
  12.9 0.6 convolution_convert_fusion
  13.5 0.8 copy-done.1
  14.3 1.5 pad_maximum_fusion
  15.8 0.0 all-gather.2.cloned.1.call-update
  15.9 0.0 reduce-scatter.7.cloned.1.call-start
  15.9 0.4 multiply_reduce_fusion.1
  16.3 65.9 %all-gather.2.cloned.1.call-done = bf16[1536,2560]{1,0:T(8,128)(2,1)} async-done(((bf16[384,2560]{1,0:T(8,128)(2,1)}), bf16[1536,2560]{1,0:T(8,128)(2,1)}) %all-gather.2.cloned.1.call-update) | async-done | bytes 7864336 | tf_op jit(solution)/shard_map/all_gather | solution.py:42
  82.2 4.1 multiply_reduce_fusion
  86.2 7.7 fusion.3
  93.9 4.4 fusion.13
  98.4 6.5 convolution_bitcast_fusion
  104.9 9.3 %copy.7 = f32[2048,1024]{1,0:T(8,128)} copy(f32[2048,1024]{0,1:T(8,128)} %convolution_bitcast_fusion) | data formatting | bytes 16777216
  114.2 0.0 copy-start.3
  114.2 0.0 reduce-scatter.7.cloned.1.call-update
  114.2 0.0 reduce-scatter.5.cloned.1.call-start
  114.3 1.3 copy-done.3
  115.6 2.2 fusion.21
  117.8 0.0 reduce-scatter.5.cloned.1.call-update
  117.8 0.0 all-reduce.2.cloned.1.call-start
  117.9 283.1 %reduce-scatter.7.cloned.1.call-done = f32[32,1024]{1,0:T(8,128)} async-done(((f32[2048,1024]{1,0:T(8,128)}), f32[32,1024]{1,0:T(8,128)}) %reduce-scatter.7.cloned.1.call-update) | async-done | bytes 131088
  401.0 1.9 copy.8
  402.8 0.0 all-reduce.2.cloned.1.call-update
  402.9 309.9 %reduce-scatter.5.cloned.1.call-done = f32[16,512]{1,0:T(8,128)} async-done(((f32[1024,512]{1,0:T(8,128)}), f32[16,512]{1,0:T(8,128)}) %reduce-scatter.5.cloned.1.call-update) | async-done | bytes 32784 | tf_op jit(solution)/shard_map/reduce_scatter | solution.py:53
  712.7 63.9 %psum.15 = f32[16,512]{1,0:T(8,128)} all-reduce(f32[16,512]{1,0:T(8,128)} %reduce-scatter.5.cloned.1.call-done), channel_id=1, replica_groups=mesh['blk'=4,'dp'=64] {'blk'}, use_global_device_ids=true, to_apply=%region_5.0 | all-reduce | flops 8192 | bytes 65536 | tf_op jit(solution)/shard_map/psum | solution.py:56
  776.6 31.6 %all-reduce.2.cloned.1.call-done = f32[32,1024]{0,1:T(8,128)} async-done(((f32[32,1024]{0,1:T(8,128)}), f32[32,1024]{0,1:T(8,128)}) %all-reduce.2.cloned.1.call-update) | async-done | bytes 131088 | tf_op jit(solution)/shard_map/psum | solution.py:56
  808.3 1.9 copy.6
Async XLA Ops:
  7.2 5.8 copy-start
  7.2 75.0 %all-gather.2.cloned.1.call-start = ((), (), s32[]{:S(2)}) async-start(), calls=%async_computation.2 | async-start | bytes 9830400 | tf_op jit(solution)/shard_map/all_gather | solution.py:42
  11.8 1.2 copy-start.2
  12.9 1.4 copy-start.1
  15.9 385.1 %reduce-scatter.7.cloned.1.call-start = ((), (), s32[]{:S(2)}) async-start(), calls=%async_computation.5 | async-start | bytes 8519680
  114.2 1.4 copy-start.3
  114.2 598.5 %reduce-scatter.5.cloned.1.call-start = ((), (), s32[]{:S(2)}) async-start(), calls=%async_computation.4 | async-start | bytes 2129920 | tf_op jit(solution)/shard_map/reduce_scatter | solution.py:53
  117.8 690.5 %all-reduce.2.cloned.1.call-start = ((), (), s32[]{:S(2)}) async-start(), calls=%async_computation.3 | async-start | bytes 1048576 | tf_op jit(solution)/shard_map/psum | solution.py:56
Sparse Core Ops, SparseCore 0:
  16.0 66.1 all-gather.1
  114.3 286.5 reduce-scatter.6
  403.5 309.2 reduce-scatter.4
  715.4 92.7 all-reduce.1
where the time goes:
time: 817 us
  waiting for transfers between devices  691 us (85%)
  blocking collectives  63.9 us (8%)
  matrix products  26 us (3%)
  local copies, waits for them, and re-layouts  16.3 us (2%)
  between operations  13.8 us (2%)
    reduce_scatter x1, waiting for transfers between devices, per_device(): lax.psum_scatter(column_product(hidden, dembed), 'dp', scatter_dimension=...  310 us
    unnamed x5, waiting for transfers between devices  283 us
    all_gather x1, waiting for transfers between devices, per_device(): lax.all_gather(packed, 'blk', axis=0, tiled=True)  65.9 us
    psum x1, blocking collectives, per_device(): grad_first, grad_second = lax.psum((first_part, second_part), 'blk')  63.9 us
    psum x1, waiting for transfers between devices, per_device(): grad_first, grad_second = lax.psum((first_part, second_part), 'blk')  31.6 us
    unnamed x11, local copies, waits for them, and re-layouts  16.3 us
  transfers between devices with their start and end apart: 4, of which 4 were waited for; matrix products, arithmetic and copies ran while one was open for 1% of the time, Pallas kernels for 0%

commit v1 on v0

--- a/solution.py
+++ b/solution.py
@@ -38,9 +38,16 @@
     embed = jnp.dot(hidden, w_second, preferred_element_type=jnp.float32).astype(jnp.bfloat16)
     mine_sqn = jnp.sum(jnp.square(fingerprints.astype(jnp.float32)), axis=1)
     packed = jnp.concatenate([fingerprints, embed], axis=1)
-    resid, other_embed = pair_tile(
-        fingerprints, embed, mine_sqn, lax.all_gather(packed, "blk", axis=0, tiled=True), width
-    )
+
+    def review_kinds(local_block):
+        return jnp.concatenate(
+            lax.all_to_all(
+                jnp.stack([local_block for _ in range(lax.axis_size("blk"))], 0), "blk", 0, 0
+            ),
+            0,
+        )
+
+    resid, other_embed = pair_tile(fingerprints, embed, mine_sqn, review_kinds(packed), width)
     summed = jnp.dot(resid, other_embed, preferred_element_type=jnp.float32)
     dembed = (summed * (2.0 / math.sqrt(group_rows * all_rows))).astype(jnp.bfloat16)
     dhidden = lax.dot_general(

time: 817 us -> 851 us (1.042)
  waiting for transfers between devices: 691 us -> 713 us
  starting transfers between devices: 0.16 us -> 8.81 us
    all_to_all x0 -> x1, waiting for transfers between devices: none -> 87.8 us  [review_kinds(): lax.all_to_all(jnp.stack([local_block for _ in range(lax.axis_size('blk')...]
    all_gather x1 -> x0, waiting for transfers between devices: 65.9 us -> none  [per_device(): lax.all_gather(packed, 'blk', axis=0, tiled=True)]
    all_to_all x0 -> x1, starting transfers between devices: none -> 8.72 us  [review_kinds(): lax.all_to_all(jnp.stack([local_block for _ in range(lax.axis_size('blk')...]
    unnamed x5 -> x4, waiting for transfers between devices: 283 us -> 283 us
where the time goes in v1:
time: 851 us
  waiting for transfers between devices  713 us (84%)
  blocking collectives  65.2 us (8%)
  matrix products  24.9 us (3%)
  local copies, waits for them, and re-layouts  20.1 us (2%)
  between operations  13.8 us (2%)
  starting transfers between devices  8.81 us (1%)
    reduce_scatter x1, waiting for transfers between devices, per_device(): lax.psum_scatter(column_product(hidden, dembed), 'dp', scatter_dimension=...  310 us
    unnamed x4, waiting for transfers between devices  283 us
    all_to_all x1, waiting for transfers between devices, review_kinds(): lax.all_to_all(jnp.stack([local_block for _ in range(lax.axis_size('blk')...  87.8 us
    psum x1, blocking collectives, per_device(): grad_first, grad_second = lax.psum((first_part, second_part), 'blk')  65.2 us
    psum x1, waiting for transfers between devices, per_device(): grad_first, grad_second = lax.psum((first_part, second_part), 'blk')  32.7 us
  transfers between devices with their start and end apart: 4, of which 4 were waited for; matrix products, arithmetic and copies ran while one was open for 1% of the time, Pallas kernels for 0%

profile of v1, /device:TPU:1, one launch (start us, length us, event | category | flops | bytes accessed | tf_op | source)
XLA Modules:
  0.0 850.5 jit_solution(11085398927850381224)
XLA Ops:
  7.2 0.0 copy-start
  7.2 4.5 fusion.22
  11.7 0.0 copy-start.2
  11.7 1.1 copy-done.2
  12.9 0.0 copy-done
  12.9 0.0 copy-start.1
  12.9 0.6 convolution_convert_fusion
  13.5 0.8 copy-done.1
  14.3 0.1 pad_maximum_fusion
  14.4 3.8 stack.2
  18.2 8.7 %all-to-all-start = ((bf16[4,384,2560]{2,1,0:T(8,128)(2,1)}), bf16[4,384,2560]{2,1,0:T(8,128)(2,1)}, u32[]{:S(2)}, u32[]{:S(2)}) async-start(bf16[4,384,2560]{2,1,0:T(8,128)(2,1)} %stack.2), calls=%async_computation | async-start | bytes 15728640 | tf_op jit(solution)/shard_map/all_to_all | solution.py:44
  26.9 0.0 reduce-scatter.7.cloned.1.call-start
  26.9 0.4 multiply_reduce_fusion.1
  27.3 87.8 %all-to-all-done = bf16[4,384,2560]{2,1,0:T(8,128)(2,1)} async-done(((bf16[4,384,2560]{2,1,0:T(8,128)(2,1)}), bf16[4,384,2560]{2,1,0:T(8,128)(2,1)}, u32[]{:S(2)}, u32[]{:S(2)}) %all-to-all-start) | async-done | bytes 7864352 | tf_op jit(solution)/shard_map/all_to_all | solution.py:44
  115.2 4.1 multiply_reduce_fusion
  119.2 6.9 fusion.3
  126.1 4.1 fusion.13
  130.3 6.5 convolution_bitcast_fusion
  136.8 9.3 %copy.10 = f32[2048,1024]{1,0:T(8,128)} copy(f32[2048,1024]{0,1:T(8,128)} %convolution_bitcast_fusion) | data formatting | bytes 16777216
  146.1 0.0 copy-start.3
  146.1 0.0 reduce-scatter.7.cloned.1.call-update
  146.1 0.0 reduce-scatter.5.cloned.1.call-start
  146.2 1.3 copy-done.3
  147.5 2.2 fusion.21
  149.7 0.0 reduce-scatter.5.cloned.1.call-update
  149.7 0.0 all-reduce.2.cloned.1.call-start
  149.8 282.7 %reduce-scatter.7.cloned.1.call-done = f32[32,1024]{1,0:T(8,128)} async-done(((f32[2048,1024]{1,0:T(8,128)}), f32[32,1024]{1,0:T(8,128)}) %reduce-scatter.7.cloned.1.call-update) | async-done | bytes 131088
  432.5 1.9 copy.11
  434.4 0.0 all-reduce.2.cloned.1.call-update
  434.4 309.8 %reduce-scatter.5.cloned.1.call-done = f32[16,512]{1,0:T(8,128)} async-done(((f32[1024,512]{1,0:T(8,128)}), f32[16,512]{1,0:T(8,128)}) %reduce-scatter.5.cloned.1.call-update) | async-done | bytes 32784 | tf_op jit(solution)/shard_map/reduce_scatter | solution.py:60
  744.2 65.2 %psum.15 = f32[16,512]{1,0:T(8,128)} all-reduce(f32[16,512]{1,0:T(8,128)} %reduce-scatter.5.cloned.1.call-done), channel_id=1, replica_groups=mesh['blk'=4,'dp'=64] {'blk'}, use_global_device_ids=true, to_apply=%region_5.0 | all-reduce | flops 8192 | bytes 65536 | tf_op jit(solution)/shard_map/psum | solution.py:63
  809.4 32.7 %all-reduce.2.cloned.1.call-done = f32[32,1024]{0,1:T(8,128)} async-done(((f32[32,1024]{0,1:T(8,128)}), f32[32,1024]{0,1:T(8,128)}) %all-reduce.2.cloned.1.call-update) | async-done | bytes 131088 | tf_op jit(solution)/shard_map/psum | solution.py:63
  842.1 1.9 copy.8
Async XLA Ops:
  7.2 5.7 copy-start
  11.7 1.2 copy-start.2
  12.9 1.4 copy-start.1
  18.2 97.0 %all-to-all-start = ((bf16[4,384,2560]{2,1,0:T(8,128)(2,1)}), bf16[4,384,2560]{2,1,0:T(8,128)(2,1)}, u32[]{:S(2)}, u32[]{:S(2)}) async-start(bf16[4,384,2560]{2,1,0:T(8,128)(2,1)} %stack.2), calls=%async_computation | async-start | bytes 15728640 | tf_op jit(solution)/shard_map/all_to_all | solution.py:44
  26.9 405.6 %reduce-scatter.7.cloned.1.call-start = ((), (), s32[]{:S(2)}) async-start(), calls=%async_computation.5 | async-start | bytes 8519680
  146.1 1.4 copy-start.3
  146.1 598.1 %reduce-scatter.5.cloned.1.call-start = ((), (), s32[]{:S(2)}) async-start(), calls=%async_computation.4 | async-start | bytes 2129920 | tf_op jit(solution)/shard_map/reduce_scatter | solution.py:60
  149.7 692.4 %all-reduce.2.cloned.1.call-start = ((), (), s32[]{:S(2)}) async-start(), calls=%async_computation.3 | async-start | bytes 1048576 | tf_op jit(solution)/shard_map/psum | solution.py:63
Sparse Core Ops, SparseCore 0:
  146.2 286.2 reduce-scatter.6
  435.0 309.1 reduce-scatter.4
  747.1 94.9 all-reduce.1
